TPU v7x, 256 devices: a whole 4x4x8 slice. The times are simulated.
256 devices in a mesh: path: 32 (over y, x, core), fac: 8 (over z).
Axes of the slice: x: 4, y: 4, z: 8, core: 2. Of those that a mesh axis runs over, the one named last changes fastest.
Arguments:
- shocks: bfloat16 [4, 2048, 8192], P(None, 'path', 'fac'), may hold values from -6 to 6
- chol_factor: bfloat16 [8192, 8192], P('path', 'fac')
- factor_vol: float32 [8192], P('fac'), may hold values from 0.3 to 1.5
- trade_loading: bfloat16 [8192, 4096], P(None, 'fac'), may hold values from -0.0625 to 0.0625
- basis_loading: bfloat16 [8192, 64], replicated, may hold values from -0.0625 to 0.0625
- trade_set: int32 [4096], P('fac'), may hold values from 0 to 4095, as said below
Outputs:
- exposure: float32 [4, 2048, 4096], P(None, 'path', 'fac')
Inputs may be any that keep to these rules, and one draw needn't show every extreme that they name: Each trade belongs to a netting set of its own block: trade_set[k] // 512 equals k // 512.
All inputs are finite; a program needn't handle non-finite values.
Results may differ from a plain program's by a relative error of at most 0.0047.
Values may be sent and summed in bfloat16 or wider, within the bound.
A program may use at most 128 MiB of HBM per device.

v0:
```python
import math

import jax
import jax.numpy as jnp
from jax import lax
from jax.sharding import PartitionSpec as P

F = 8192
NSETS = 4096


def solve_step(gram, moment, basis, total_paths):
    ridged = gram + 0.01 * total_paths * jnp.eye(gram.shape[0], dtype=jnp.float32)
    factor = jnp.linalg.cholesky(ridged)
    coef = jax.scipy.linalg.cho_solve((factor, True), moment)
    predicted = jnp.dot(
        basis, coef, precision=lax.Precision.HIGHEST, preferred_element_type=jnp.float32
    )
    return jnp.maximum(predicted, 0.0)


def on_device(shocks, chol_factor, factor_vol, trade_loading, basis_loading, trade_set):
    step_count, path_count, fac_width = shocks.shape
    row_count = step_count * path_count
    flat_shocks = shocks.reshape(row_count, fac_width)
    factor_share = F // lax.axis_size("fac")
    contract_last = (((1,), (1,)), ((), ()))
    full_rows = lax.all_gather(chol_factor, "path", axis=0, tiled=True)
    increments = lax.psum_scatter(
        lax.dot_general(full_rows, flat_shocks, contract_last, preferred_element_type=jnp.float32),
        "fac",
        scatter_dimension=0,
        tiled=True,
    )
    scaled = increments.reshape(factor_share, step_count, path_count) * (
        factor_vol[:, None, None] / math.sqrt(step_count)
    )
    levels = jnp.cumsum(scaled, axis=1).astype(jnp.bfloat16).reshape(factor_share, row_count)
    basis_count = basis_loading.shape[1]
    contract_first = (((0,), (0,)), ((), ()))
    piece = lax.all_gather(levels, "fac", axis=0, tiled=True)
    trade_sum = lax.dot_general(
        piece, trade_loading, contract_first, preferred_element_type=jnp.float32
    )
    basis_sum = lax.dot_general(
        piece, basis_loading, contract_first, preferred_element_type=jnp.float32
    )
    values = jax.nn.softplus(trade_sum) - 1.0
    sets_here = NSETS // lax.axis_size("fac")
    local_set = trade_set % sets_here
    member = (local_set[:, None] == jnp.arange(sets_here, dtype=jnp.int32)[None, :]).astype(
        jnp.float32
    )
    netting = jnp.dot(
        values, member, precision=lax.Precision.HIGHEST, preferred_element_type=jnp.float32
    )
    basis = jnp.tanh(basis_sum).reshape(step_count, path_count, basis_count)
    netting = netting.reshape(step_count, path_count, sets_here)
    gram = jnp.einsum(
        "tpm,tpn->tmn",
        basis,
        basis,
        precision=lax.Precision.HIGHEST,
        preferred_element_type=jnp.float32,
    )
    moment = jnp.einsum(
        "tpm,tpn->tmn",
        basis,
        netting,
        precision=lax.Precision.HIGHEST,
        preferred_element_type=jnp.float32,
    )
    total_paths = path_count * lax.axis_size("path")
    results = []
    for step in range(step_count):
        gram_total, moment_total = lax.psum((gram[step], moment[step]), "path")
        results.append(solve_step(gram_total, moment_total, basis[step], total_paths))
    return jnp.stack(results)


def solution(mesh):
    in_specs = (P(None, "path", "fac"), P("path", "fac"), P("fac"), P(None, "fac"), P(), P("fac"))
    out_specs = P(None, "path", "fac")
    return jax.shard_map(
        on_device, mesh=mesh, in_specs=in_specs, out_specs=out_specs, check_vma=False
    )
```

profile of v0, /device:TPU:1, one launch (start us, length us, event | category | flops | bytes accessed | tf_op | source)
XLA Modules:
  0.0 512.1 jit_solution(6052345440305277966)
XLA Ops:
  7.3 84.4 %all-gather.3.cloned.1.call-done = bf16[8192,1024]{1,0:T(8,128)(2,1)} async-done(((bf16[256,1024]{1,0:T(8,128)(2,1)}), bf16[8192,1024]{1,0:T(8,128)(2,1)}) %all-gather.3.cloned.1.call-update) | async-done | bytes 16777232 | tf_op jit(solution)/shard_map/all_gather | solution.py:28
  91.7 13.6 %fusion.53 = f32[8192,256]{1,0:T(8,128)} fusion(bf16[8192,1024]{1,0:T(8,128)(2,1)} %all-gather.3.cloned.1.call-done, bf16[256,1024]{1,0:T(8,128)(2,1)} %bitcast.96), kind=kOutput, calls=%fused_computation.96 | convolution fusion | flops 4294967296 | bytes 25690112 | tf_op jit(solution)/shard_map/dot_general | solution.py:30
  106.0 93.5 %reduce-scatter.2.cloned.1.call-done = f32[1024,256]{1,0:T(8,128)} async-done(((f32[8192,256]{1,0:T(8,128)}), f32[1024,256]{1,0:T(8,128)}) %reduce-scatter.2.cloned.1.call-update) | async-done | bytes 1048592 | tf_op jit(solution)/shard_map/reduce_scatter | solution.py:29
  199.5 1.6 copy.18
  201.0 0.9 reduce-window_convert_fusion
  202.0 53.4 %all-gather.5.cloned.1.call-done = bf16[8192,256]{0,1:T(8,128)(2,1)} async-done(((bf16[1024,256]{0,1:T(8,128)(2,1)}), bf16[8192,256]{0,1:T(8,128)(2,1)}) %all-gather.5.cloned.1.call-update) | async-done | bytes 4194320 | tf_op jit(solution)/shard_map/all_gather | solution.py:41
  255.4 3.6 convolution_tanh_fusion
  259.4 7.0 %fusion.54 = f32[256,512]{1,0:T(8,128)S(1)} fusion(bf16[8192,256]{0,1:T(8,128)(2,1)} %all-gather.5.cloned.1.call-done, bf16[8192,512]{1,0:T(8,128)(2,1)} %param.12), kind=kOutput, calls=%fused_computation.97 | convolution fusion | flops 2147483648 | bytes 13107200 | tf_op jit(solution)/shard_map/dot_general | solution.py:42
  266.4 1.0 fusion.5
  269.7 109.4 %all-reduce.5.cloned.1.call-done = (f32[64,64]{0,1:T(8,128)}, f32[64,64]{0,1:T(8,128)}, f32[64,64]{0,1:T(8,128)}, f32[64,64]{0,1:T(8,128)}) async-done(((f32[64,64]{0,1:T(8,128)}, f32[64,64]{0,1:T(8,128)}, f32[64,64]{0,1:T(8,128)}, f32[64,64]{0,1:T(8,128)}), (f32[64,64]{0,1:T(8,128)}, f32[64,64]{0,1:T(8,128)}, f32[64,64]{0,1:T(8,128)}, f32[64,64]{0,1:T(8,128)})) %all-reduce.5.cloned.1.call-update) | async-done | bytes 65552 | tf_op jit(solution)/shard_map/psum | solution.py:76
  380.8 5.8 %cholesky.107 = f32[64,64]{1,0:T(8,128)S(1)} custom-call(f32[64,64]{1,0:T(8,128)S(1)} %fusion.34), custom_call_target="Cholesky" | custom-call | tf_op jit(solution)/shard_map/jit(cholesky)/cholesky | solution.py:14
  388.7 5.8 %cholesky.96 = f32[64,64]{1,0:T(8,128)S(1)} custom-call(f32[64,64]{1,0:T(8,128)S(1)} %fusion.39), custom_call_target="Cholesky" | custom-call | tf_op jit(solution)/shard_map/jit(cholesky)/cholesky | solution.py:14
  397.7 5.8 %cholesky.85 = f32[64,64]{1,0:T(8,128)S(1)} custom-call(f32[64,64]{1,0:T(8,128)S(1)} %fusion.44), custom_call_target="Cholesky" | custom-call | tf_op jit(solution)/shard_map/jit(cholesky)/cholesky | solution.py:14
  405.8 5.8 %cholesky.74 = f32[64,64]{1,0:T(8,128)S(1)} custom-call(f32[64,64]{1,0:T(8,128)S(1)} %fusion.49), custom_call_target="Cholesky" | custom-call | tf_op jit(solution)/shard_map/jit(cholesky)/cholesky | solution.py:14
  412.3 4.9 custom-call.13
  417.2 4.9 custom-call.12
  422.1 4.9 custom-call.11
  427.7 4.9 custom-call.10
  432.6 64.7 %all-reduce.7.cloned.1.call-done = (f32[64,512]{1,0:T(8,128)}, f32[64,512]{1,0:T(8,128)}, f32[64,512]{1,0:T(8,128)}, f32[64,512]{1,0:T(8,128)}) async-done(((f32[64,512]{1,0:T(8,128)}, f32[64,512]{1,0:T(8,128)}, f32[64,512]{1,0:T(8,128)}, f32[64,512]{1,0:T(8,128)}), (f32[64,512]{1,0:T(8,128)}, f32[64,512]{1,0:T(8,128)}, f32[64,512]{1,0:T(8,128)}, f32[64,512]{1,0:T(8,128)})) %all-reduce.7.cloned.1.call-update) | async-done | bytes 524304 | tf_op jit(solution)/shard_map/psum | solution.py:76
  497.3 1.2 fusion.32
  499.2 1.2 fusion.37
  501.0 1.2 fusion.42
  502.9 1.2 fusion.47
  504.7 0.8 pad_maximum_fusion
  (53 shorter events, 17.0 us)
Async XLA Ops:
  6.5 248.8 %copy-start = (bf16[8192,64]{0,1:T(8,128)(2,1)S(1)}, bf16[8192,64]{0,1:T(8,128)(2,1)}, u32[]{:S(2)}) copy-start(bf16[8192,64]{0,1:T(8,128)(2,1)} %param.13) | copy-start | bytes 3145732
  6.5 85.1 %all-gather.3.cloned.1.call-start = ((), (), s32[]{:S(2)}) async-start(), calls=%async_computation.1 | async-start | bytes 17301504 | tf_op jit(solution)/shard_map/all_gather | solution.py:28
  7.3 192.2 %reduce-scatter.2.cloned.1.call-start = ((), (), s32[]{:S(2)}) async-start(), calls=%async_computation.2 | async-start | bytes 9437184 | tf_op jit(solution)/shard_map/reduce_scatter | solution.py:29
  105.3 0.7 copy-start.1
  105.3 96.7 %copy-start.2 = (s32[512]{0:T(512)S(1)}, s32[512]{0:T(512)}, u32[]{:S(2)}) copy-start(s32[512]{0:T(512)} %param.14) | copy-start | bytes 6148
  105.3 150.1 %all-gather.5.cloned.1.call-start = ((), (), s32[]{:S(2)}) async-start(), calls=%async_computation.3 | async-start | bytes 4718592 | tf_op jit(solution)/shard_map/all_gather | solution.py:41
  201.9 177.2 %all-reduce.5.cloned.1.call-start = ((), (), s32[]{:S(2)}) async-start(), calls=%async_computation.4 | async-start | bytes 262144 | tf_op jit(solution)/shard_map/psum | solution.py:76
  268.7 228.6 %all-reduce.7.cloned.1.call-start = ((), (), s32[]{:S(2)}) async-start(), calls=%async_computation.5 | async-start | bytes 1048576 | tf_op jit(solution)/shard_map/psum | solution.py:76
Sparse Core Ops, SparseCore 0:
  9.9 81.7 all-gather.2
  105.4 93.9 reduce-scatter.1
  202.0 53.2 all-gather.4
  268.8 110.3 all-reduce.4
  382.4 114.8 all-reduce.6
where the time goes:
time: 513 us; the launch traced here: 512 us
  waiting for transfers between devices  406 us (79%)
  other arithmetic  54.8 us (11%)
  matrix products  33.4 us (7%)
  between operations  13.4 us (3%)
    psum x2, waiting for transfers between devices, on_device(): gram_total, moment_total = lax.psum((gram[step], moment[step]), 'path')  174 us
    reduce_scatter x1, waiting for transfers between devices, on_device(): lax.psum_scatter(lax.dot_general(full_rows, flat_shocks, contract_last, p...  93.5 us
    all_gather x1, waiting for transfers between devices, on_device(): full_rows = lax.all_gather(chol_factor, 'path', axis=0, tiled=True)  84.4 us
    all_gather x1, waiting for transfers between devices, on_device(): piece = lax.all_gather(levels, 'fac', axis=0, tiled=True)  53.4 us
    another operation x12, other arithmetic, solve_step(): factor = jnp.linalg.cholesky(ridged)  26.2 us
    another operation x8, other arithmetic, solve_step(): coef = jax.scipy.linalg.cho_solve((factor, True), moment)  22.1 us
    dot_general x1, matrix products, on_device(): lax.dot_general(full_rows, flat_shocks, contract_last, preferred_element_...  13.6 us
  transfers between devices with their start and end apart: 5, of which 5 were waited for; matrix products, arithmetic and copies ran while one was open for 11% of the time, Pallas kernels for 0%

commit v1 on v0

v1 whole, which is shorter than its diff:
```python
import functools
import math

import jax
import jax.numpy as jnp
from jax import lax
from jax.experimental import pallas as pl
from jax.experimental.pallas import tpu as pltpu
from jax.sharding import PartitionSpec as P

F = 8192
NSETS = 4096
MESH = pl.DeviceIdType.MESH
HIGH = lax.Precision.HIGHEST


def split_dot(a, b):
    high = a.astype(jnp.bfloat16)
    low = (a - high.astype(jnp.float32)).astype(jnp.bfloat16)
    both = jnp.dot(
        jnp.concatenate([high, low], axis=0), b, preferred_element_type=jnp.float32
    )
    rows = a.shape[0]
    return both[:rows] + both[rows:]


def invert(mats):
    n = mats[0].shape[0]
    count = len(mats)
    row = lax.broadcasted_iota(jnp.int32, (n, 2 * n), 0)
    lane = lax.broadcasted_iota(jnp.int32, (n, 2 * n), 1)
    eye = jnp.where(lane == row + n, 1.0, 0.0)
    wide = [jnp.concatenate([m, jnp.zeros_like(m)], axis=1) + eye for m in mats]
    blocks = tuple(tuple(w[8 * b : 8 * b + 8] for b in range(n // 8)) for w in wide)
    sub = lax.broadcasted_iota(jnp.int32, (8, 1), 0)

    def body(_, blocks):
        done = []
        for m in range(count):
            rows = list(blocks[m])
            for k in range(8):
                pivot_row = rows[0][k : k + 1, :]
                inverse = 1.0 / pivot_row[:, k : k + 1]
                scaled = pivot_row * inverse
                fresh = []
                for b in range(n // 8):
                    col = rows[b][:, k : k + 1]
                    if b == 0:
                        col = jnp.where(sub == k, col - 1.0, col)
                    fresh.append(rows[b] - col * scaled)
                rows = fresh
            rows = rows[1:] + rows[:1]
            done.append(tuple(pltpu.roll(r, 2 * n - 8, 1) for r in rows))
        return tuple(done)

    blocks = lax.fori_loop(0, n // 8, body, blocks)
    return [jnp.concatenate(b, axis=0)[:, :n] for b in blocks]


def tail_kernel(
    group, total_paths, drive_ref, proj_ref, member_ref, out_ref,
    part, landed, total, base, send_a, recv_a, send_b, recv_b,
):
    me = lax.axis_index("path")
    barrier = pltpu.get_barrier_semaphore()

    @pl.loop(1, group)
    def _(d):
        pl.semaphore_signal(
            barrier, inc=1, device_id={"path": lax.rem(me + d, group)}, device_id_type=MESH
        )

    steps, paths, sets = drive_ref.shape
    nb = proj_ref.shape[2]
    contract = (((0,), (0,)), ((), ()))
    for t in range(steps):
        v = drive_ref[t]
        values = jnp.maximum(v, 0.0) + jnp.log(1.0 + jnp.exp(-jnp.abs(v))) - 1.0
        basis = jnp.tanh(proj_ref[t])
        base[t] = basis
        moment = lax.dot_general(
            basis, values, contract, precision=HIGH, preferred_element_type=jnp.float32
        )
        gram = lax.dot_general(
            basis, basis, contract, precision=HIGH, preferred_element_type=jnp.float32
        )
        gram = jnp.concatenate([gram, jnp.zeros_like(gram)], axis=1)
        at = pl.ds(t * nb // 8, nb // 8)
        part[at, :, 0:sets] = moment.reshape(nb // 8, 8, sets)
        part[at, :, sets : sets + 2 * nb] = gram.reshape(nb // 8, 8, 2 * nb)

    pl.semaphore_wait(barrier, group - 1)

    def out_copy(d):
        to = lax.rem(me + d, group)
        return pltpu.make_async_remote_copy(
            src_ref=part.at[to], dst_ref=landed.at[me], send_sem=send_a.at[to],
            recv_sem=recv_a.at[me], device_id={"path": to}, device_id_type=MESH,
        )

    def in_copy(d):
        source = lax.rem(me + d, group)
        return pltpu.make_async_remote_copy(
            src_ref=part.at[source], dst_ref=landed.at[source], send_sem=send_a.at[source],
            recv_sem=recv_a.at[source], device_id={"path": source}, device_id_type=MESH,
        )

    @pl.loop(1, group)
    def _(d):
        out_copy(d).start()

    landed[me] = part[me]

    @pl.loop(1, group)
    def _(d):
        in_copy(d).wait()

    mine = jnp.sum(landed[...], axis=0)
    total[me, :, 0:sets] = split_dot(mine[:, 0:sets], member_ref[...])
    total[me, :, sets : sets + 2 * nb] = mine[:, sets : sets + 2 * nb]

    def share_copy(d):
        to = lax.rem(me + d, group)
        return pltpu.make_async_remote_copy(
            src_ref=total.at[me], dst_ref=total.at[me], send_sem=send_b.at[to],
            recv_sem=recv_b.at[me], device_id={"path": to}, device_id_type=MESH,
        )

    def taken_copy(d):
        source = lax.rem(me + d, group)
        return pltpu.make_async_remote_copy(
            src_ref=total.at[source], dst_ref=total.at[source], send_sem=send_b.at[source],
            recv_sem=recv_b.at[source], device_id={"path": source}, device_id_type=MESH,
        )

    @pl.loop(1, group)
    def _(d):
        share_copy(d).start()

    @pl.loop(1, group)
    def _(d):
        taken_copy(d).wait()

    row = lax.broadcasted_iota(jnp.int32, (nb, nb), 0)
    lane = lax.broadcasted_iota(jnp.int32, (nb, nb), 1)
    ridge = jnp.where(row == lane, 0.01 * total_paths, 0.0)
    grams = [
        total[t * nb // 8 : (t + 1) * nb // 8, :, sets : sets + nb].reshape(nb, nb) + ridge
        for t in range(steps)
    ]
    inverses = invert(grams)
    for t in range(steps):
        weight = jnp.dot(
            base[t], inverses[t], precision=HIGH, preferred_element_type=jnp.float32
        )
        moment = total[t * nb // 8 : (t + 1) * nb // 8, :, 0:sets].reshape(nb, sets)
        predicted = jnp.dot(
            weight, moment, precision=HIGH, preferred_element_type=jnp.float32
        )
        out_ref[t] = jnp.maximum(predicted, 0.0)


def tail(drive, proj, member, total_paths):
    group = lax.axis_size("path")
    steps, paths, sets = drive.shape
    nb = proj.shape[2]
    rows = steps * nb // 8
    width = sets + 2 * nb
    vmem = pl.BlockSpec(memory_space=pltpu.VMEM)
    return pl.pallas_call(
        functools.partial(tail_kernel, group, total_paths),
        out_shape=jax.ShapeDtypeStruct(drive.shape, jnp.float32),
        in_specs=[vmem] * 3,
        out_specs=vmem,
        scratch_shapes=[
            pltpu.VMEM((rows, 8, width), jnp.float32),
            pltpu.VMEM((group, 8, width), jnp.float32),
            pltpu.VMEM((rows, 8, width), jnp.float32),
            pltpu.VMEM((steps, paths, nb), jnp.float32),
            pltpu.SemaphoreType.DMA((group,)),
            pltpu.SemaphoreType.DMA((group,)),
            pltpu.SemaphoreType.DMA((group,)),
            pltpu.SemaphoreType.DMA((group,)),
        ],
        compiler_params=pltpu.CompilerParams(collective_id=1, has_side_effects=True),
    )(drive, proj, member)


def on_device(shocks, chol_factor, factor_vol, trade_loading, basis_loading, trade_set):
    step_count, path_count, fac_width = shocks.shape
    row_count = step_count * path_count
    flat_shocks = shocks.reshape(row_count, fac_width)
    factor_share = F // lax.axis_size("fac")
    contract_last = (((1,), (1,)), ((), ()))
    full_rows = lax.all_gather(chol_factor, "path", axis=0, tiled=True)
    increments = lax.psum_scatter(
        lax.dot_general(full_rows, flat_shocks, contract_last, preferred_element_type=jnp.float32),
        "fac",
        scatter_dimension=0,
        tiled=True,
    )
    scaled = increments.reshape(factor_share, step_count, path_count) * (
        factor_vol[:, None, None] / math.sqrt(step_count)
    )
    levels = jnp.cumsum(scaled, axis=1).astype(jnp.bfloat16).reshape(factor_share, row_count)
    basis_count = basis_loading.shape[1]
    contract_first = (((0,), (0,)), ((), ()))
    piece = lax.all_gather(levels, "fac", axis=0, tiled=True)
    trade_sum = lax.dot_general(
        piece, trade_loading, contract_first, preferred_element_type=jnp.float32
    )
    basis_sum = lax.dot_general(
        piece, basis_loading, contract_first, preferred_element_type=jnp.float32
    )
    sets_here = NSETS // lax.axis_size("fac")
    local_set = trade_set % sets_here
    member = (local_set[:, None] == jnp.arange(sets_here, dtype=jnp.int32)[None, :]).astype(
        jnp.bfloat16
    )
    drive = trade_sum.reshape(step_count, path_count, -1)
    proj = basis_sum.reshape(step_count, path_count, basis_count)
    return tail(drive, proj, member, path_count * lax.axis_size("path"))


def solution(mesh):
    in_specs = (P(None, "path", "fac"), P("path", "fac"), P("fac"), P(None, "fac"), P(), P("fac"))
    out_specs = P(None, "path", "fac")
    return jax.shard_map(
        on_device, mesh=mesh, in_specs=in_specs, out_specs=out_specs, check_vma=False
    )
```

time: 513 us -> 313 us (0.61)
  waiting for transfers between devices: 406 us -> 231 us
  other arithmetic: 54.8 us -> 1.85 us
  Pallas kernels: 0 us -> 37.5 us
  matrix products: 33.4 us -> 25.4 us
    psum x2 -> x0, waiting for transfers between devices: 174 us -> none  [on_device(): gram_total, moment_total = lax.psum((gram[step], moment[step]), 'path')]
    another operation x21 -> x0, other arithmetic: 49.2 us -> none  [the longest x12 26.2 us: solve_step(): factor = jnp.linalg.cholesky(ridged)]
    pallas_call x0 -> x1, Pallas kernels: none -> 37.5 us  [tail(): pl.pallas_call(functools.partial(tail_kernel, group, total_paths), out_sh...]
    another operation x8 -> x0, matrix products: 5.92 us -> none  [solve_step(): coef = jax.scipy.linalg.cho_solve((factor, True), moment)]
  transfers between devices with their start and end apart: 5 -> 3, of which waited for: 5 -> 3; matrix products, arithmetic and copies ran while one was open for 11% -> 0% of each run, Pallas kernels for 0% -> 0%
where the time goes in v1:
time: 313 us
  waiting for transfers between devices  231 us (74%)
  Pallas kernels  37.5 us (12%)
  matrix products  25.4 us (8%)
  between operations  13.1 us (4%)
  local copies, waits for them, and re-layouts  4.04 us (1%)
    reduce_scatter x1, waiting for transfers between devices, on_device(): lax.psum_scatter(lax.dot_general(full_rows, flat_shocks, contract_last, p...  93.5 us
    all_gather x1, waiting for transfers between devices, on_device(): full_rows = lax.all_gather(chol_factor, 'path', axis=0, tiled=True)  84.4 us
    all_gather x1, waiting for transfers between devices, on_device(): piece = lax.all_gather(levels, 'fac', axis=0, tiled=True)  52.5 us
    pallas_call x1, Pallas kernels, tail(): pl.pallas_call(functools.partial(tail_kernel, group, total_paths), out_sh...  37.5 us
    dot_general x1, matrix products, on_device(): lax.dot_general(full_rows, flat_shocks, contract_last, preferred_element_...  13.6 us
    dot_general x1, matrix products, on_device(): lax.dot_general(piece, trade_loading, contract_first, preferred_element_t...  7.78 us
  transfers between devices with their start and end apart: 3, of which 3 were waited for; matrix products, arithmetic and copies ran while one was open for 0% of the time, Pallas kernels for 0%

profile of v1, /device:TPU:1, one launch (start us, length us, event | category | flops | bytes accessed | tf_op | source)
XLA Modules:
  0.0 313.1 jit_solution(16207742597354296493)
XLA Ops:
  6.5 0.0 copy-start
  6.5 0.0 all-gather.3.cloned.1.call-start
  6.5 0.7 all-gather.3.cloned.1.call-update
  7.3 0.0 reduce-scatter.2.cloned.1.call-start
  7.3 84.4 %all-gather.3.cloned.1.call-done = bf16[8192,1024]{1,0:T(8,128)(2,1)} async-done(((bf16[256,1024]{1,0:T(8,128)(2,1)}), bf16[8192,1024]{1,0:T(8,128)(2,1)}) %all-gather.3.cloned.1.call-update) | async-done | bytes 16777232 | tf_op jit(solution)/shard_map/all_gather | solution.py:195
  91.7 13.6 %fusion.4 = f32[8192,256]{1,0:T(8,128)} fusion(bf16[8192,1024]{1,0:T(8,128)(2,1)} %all-gather.3.cloned.1.call-done, bf16[256,1024]{1,0:T(8,128)(2,1)} %bitcast.15), kind=kOutput, calls=%fused_computation.10 | convolution fusion | flops 4294967296 | bytes 25690112 | tf_op jit(solution)/shard_map/dot_general | solution.py:197
  105.3 0.0 copy-start.1
  105.3 0.0 copy-start.2
  105.3 0.0 reduce-scatter.2.cloned.1.call-update
  105.3 0.0 all-gather.5.cloned.1.call-start
  105.4 0.6 copy-done.1
  106.0 93.5 %reduce-scatter.2.cloned.1.call-done = f32[1024,256]{1,0:T(8,128)} async-done(((f32[8192,256]{1,0:T(8,128)}), f32[1024,256]{1,0:T(8,128)}) %reduce-scatter.2.cloned.1.call-update) | async-done | bytes 1048592 | tf_op jit(solution)/shard_map/reduce_scatter | solution.py:196
  199.5 1.6 copy.8
  201.0 0.9 reduce-window_convert_fusion
  201.9 0.0 all-gather.5.cloned.1.call-update
  201.9 0.0 copy-done.2
  202.0 1.0 fusion.1.member_ref
  202.9 52.5 %all-gather.5.cloned.1.call-done = bf16[8192,256]{0,1:T(8,128)(2,1)} async-done(((bf16[1024,256]{0,1:T(8,128)(2,1)}), bf16[8192,256]{0,1:T(8,128)(2,1)}) %all-gather.5.cloned.1.call-update) | async-done | bytes 4194320 | tf_op jit(solution)/shard_map/all_gather | solution.py:208
  255.4 0.0 copy-done
  255.4 4.1 %fusion.6 = f32[256,64]{1,0:T(8,128)} fusion(bf16[8192,256]{0,1:T(8,128)(2,1)} %all-gather.5.cloned.1.call-done, bf16[8192,64]{0,1:T(8,128)(2,1)S(1)} %copy-done), kind=kOutput, calls=%fused_computation.12 | convolution fusion | flops 268435456 | bytes 5308416 | tf_op jit(solution)/shard_map/dot_general | solution.py:212
  259.4 7.8 %fusion.5 = f32[256,512]{1,0:T(8,128)} fusion(bf16[8192,256]{0,1:T(8,128)(2,1)} %all-gather.5.cloned.1.call-done, bf16[8192,512]{1,0:T(8,128)(2,1)} %param.9), kind=kOutput, calls=%fused_computation.11 | convolution fusion | flops 2147483648 | bytes 13107200 | tf_op jit(solution)/shard_map/dot_general | solution.py:209
  267.2 37.5 %shard_map.64 = f32[4,64,512]{2,1,0:T(8,128)} custom-call(f32[4,64,512]{2,1,0:T(8,128)} %bitcast.13, f32[4,64,64]{2,1,0:T(8,128)} %bitcast.14, bf16[512,512]{1,0:T(8,128)(2,1)} %fusion.1.member_ref), custom_call_target="tpu_custom_call" | custom-call | tf_op jit(solution)/shard_map/pallas_call | solution.py:170
  304.7 1.9 copy.12
  (2 shorter events, 0.0 us)
Async XLA Ops:
  6.5 248.8 %copy-start = (bf16[8192,64]{0,1:T(8,128)(2,1)S(1)}, bf16[8192,64]{0,1:T(8,128)(2,1)}, u32[]{:S(2)}) copy-start(bf16[8192,64]{0,1:T(8,128)(2,1)} %param.10) | copy-start | bytes 3145732
  6.5 85.1 %all-gather.3.cloned.1.call-start = ((), (), s32[]{:S(2)}) async-start(), calls=%async_computation.1 | async-start | bytes 17301504 | tf_op jit(solution)/shard_map/all_gather | solution.py:195
  7.3 192.2 %reduce-scatter.2.cloned.1.call-start = ((), (), s32[]{:S(2)}) async-start(), calls=%async_computation.2 | async-start | bytes 9437184 | tf_op jit(solution)/shard_map/reduce_scatter | solution.py:196
  105.3 0.7 copy-start.1
  105.3 96.7 %copy-start.2 = (s32[512]{0:T(512)S(1)}, s32[512]{0:T(512)}, u32[]{:S(2)}) copy-start(s32[512]{0:T(512)} %param.11) | copy-start | bytes 6148
  105.3 150.1 %all-gather.5.cloned.1.call-start = ((), (), s32[]{:S(2)}) async-start(), calls=%async_computation.3 | async-start | bytes 4718592 | tf_op jit(solution)/shard_map/all_gather | solution.py:208
Sparse Core Ops, SparseCore 0:
  9.9 81.7 all-gather.2
  105.4 93.9 reduce-scatter.1
  202.0 53.2 all-gather.4

commit v2 on v1

--- a/solution.py
+++ b/solution.py
@@ -8,7 +8,6 @@
 from jax.experimental.pallas import tpu as pltpu
 from jax.sharding import PartitionSpec as P
 
-F = 8192
 NSETS = 4096
 MESH = pl.DeviceIdType.MESH
 HIGH = lax.Precision.HIGHEST
@@ -73,10 +72,13 @@
     steps, paths, sets = drive_ref.shape
     nb = proj_ref.shape[2]
     contract = (((0,), (0,)), ((), ()))
+    v = jnp.zeros(drive_ref.shape[1:], jnp.float32)
+    w = jnp.zeros(proj_ref.shape[1:], jnp.float32)
     for t in range(steps):
-        v = drive_ref[t]
+        v = v + drive_ref[t]
+        w = w + proj_ref[t]
         values = jnp.maximum(v, 0.0) + jnp.log(1.0 + jnp.exp(-jnp.abs(v))) - 1.0
-        basis = jnp.tanh(proj_ref[t])
+        basis = jnp.tanh(w)
         base[t] = basis
         moment = lax.dot_general(
             basis, values, contract, precision=HIGH, preferred_element_type=jnp.float32
@@ -186,39 +188,422 @@
     )(drive, proj, member)
 
 
+def push(src, dst, send_sem, recv_sem, where):
+    return pltpu.make_async_remote_copy(
+        src_ref=src, dst_ref=dst, send_sem=send_sem, recv_sem=recv_sem,
+        device_id=where, device_id_type=MESH,
+    )
+
+
+def rises(s):
+    extra = [0, 1, 3, 3, 0, 1, 1, 0]
+    total = 2
+    for at, more in enumerate(extra):
+        if more:
+            total = total + jnp.where(s == at, more, 0)
+    return total
+
+
+def front_kernel(
+    planes, group, scale, chol_ref, shock_hbm, vol_ref, trade_hbm, basis_ref, drive_ref, proj_ref,
+    turned, slices, shocks, vols, loads, full, acc,
+    local_sem, a_send, a_recv, v_send, v_recv, s_up, s_down, s_recv,
+    c_up, c_down, c_recv, g_send, g_recv,
+):
+    me = lax.axis_index("path")
+    z = lax.axis_index("fac")
+    above, below = {"fac": lax.rem(z + 1, planes)}, {"fac": lax.rem(z + planes - 1, planes)}
+    per_plane = group // planes
+    height, cols = chol_ref.shape
+    width = cols // group
+    sets = trade_hbm.shape[1]
+    nb = basis_ref.shape[1]
+    half_rows = shock_hbm.shape[0] // 2
+
+    barrier = pltpu.get_barrier_semaphore()
+
+    @pl.loop(1, group)
+    def _(d):
+        pl.semaphore_signal(
+            barrier, inc=1, device_id={"path": lax.rem(me + d, group)}, device_id_type=MESH
+        )
+
+    @pl.loop(1, planes)
+    def _(d):
+        pl.semaphore_signal(
+            barrier, inc=1, device_id={"fac": lax.rem(z + d, planes)}, device_id_type=MESH
+        )
+
+    load_trades = pltpu.make_async_copy(trade_hbm, loads.at[:, 0:sets], local_sem.at[0])
+    load_trades.start()
+    load_shocks = [
+        pltpu.make_async_copy(
+            shock_hbm.at[pl.ds(h * half_rows, half_rows)], shocks.at[z, h], local_sem.at[1 + h]
+        )
+        for h in range(2)
+    ]
+    for copy in load_shocks:
+        copy.start()
+
+    for b in range(cols // 128):
+        block = chol_ref[:, 128 * b : 128 * (b + 1)].T
+        at = pl.ds(b * (128 // width), 128 // width)
+        turned[at] = block.reshape(128 // width, width, height)
+    vols[z] = vol_ref[...]
+    for copy in load_shocks:
+        copy.wait()
+
+    pl.semaphore_wait(barrier, group - 1 + planes - 1)
+
+    def shock_up(s, h):
+        return push(shocks.at[s, h], shocks.at[s, h], s_up.at[s * 2 + h], s_recv.at[s * 2 + h], above)
+
+    def shock_down(s, h):
+        return push(
+            shocks.at[s, h], shocks.at[s, h], s_down.at[s * 2 + h], s_recv.at[s * 2 + h], below
+        )
+
+    def up_source(k):
+        return lax.rem(z + planes - k, planes)
+
+    def down_source(k):
+        return lax.rem(z + k, planes)
+
+    for h in range(2):
+        shock_up(z, h).start()
+        shock_down(z, h).start()
+
+    def vol_copy(d):
+        to = lax.rem(z + d, planes)
+        return push(vols.at[z], vols.at[z], v_send.at[to], v_recv.at[z], {"fac": to})
+
+    def vol_taken(d):
+        source = lax.rem(z + d, planes)
+        return push(
+            vols.at[source], vols.at[source], v_send.at[source], v_recv.at[source], {"fac": source}
+        )
+
+    @pl.loop(1, planes)
+    def _(d):
+        vol_copy(d).start()
+
+    def slice_copy(d):
+        to = lax.rem(me + d, group)
+        return push(turned.at[to], slices.at[me, z], a_send.at[to], a_recv.at[me], {"path": to})
+
+    def slice_taken(source):
+        return push(
+            turned.at[source], slices.at[source, z], a_send.at[source], a_recv.at[source],
+            {"path": source},
+        )
+
+    @pl.when(me >= per_plane * z)
+    def _():
+        @pl.loop(1, group)
+        def _(d):
+            slice_copy(d).start()
+
+        slices[me, z] = turned[me]
+
+    @pl.loop(1, planes)
+    def _(d):
+        vol_taken(d).wait_recv()
+
+    load_trades.wait()
+    vol_rows = vols[...].reshape(planes * vol_ref.shape[0], 128) * scale
+    vol_rows = jnp.concatenate(
+        [vol_rows, jnp.zeros((128 - vol_rows.shape[0], 128), jnp.float32)], axis=0
+    )
+
+    def scale_rows(c, columns):
+        column = columns[:, 0:1]
+        at = pl.ds(pl.multiple_of(c * 128, 128), 128)
+        loads[at, 0:sets] = (loads[at, 0:sets].astype(jnp.float32) * column).astype(jnp.bfloat16)
+        basis = basis_ref[at, :].astype(jnp.float32) * column
+        high = basis.astype(jnp.bfloat16)
+        low = (basis - high.astype(jnp.float32)).astype(jnp.bfloat16)
+        loads[at, sets : sets + 2 * nb] = jnp.concatenate([high, low], axis=1)
+        return pltpu.roll(columns, 127, 1)
+
+    lax.fori_loop(0, loads.shape[0] // 128, scale_rows, vol_rows.T)
+
+    @pl.loop(1, group)
+    def _(d):
+        source = lax.rem(me + d, group)
+
+        @pl.when(source >= per_plane * z)
+        def _():
+            slice_taken(source).wait_recv()
+
+    def part(s, g):
+        return slices.at[pl.ds(g * per_plane, per_plane), s]
+
+    def slice_up(s, g):
+        return push(part(s, g), part(s, g), c_up.at[s * planes + g], c_recv.at[s * planes + g], above)
+
+    def slice_down(s, g):
+        return push(
+            part(s, g), part(s, g), c_down.at[s * planes + g], c_recv.at[s * planes + g], below
+        )
+
+    @pl.loop(0, planes)
+    def _(g):
+        @pl.when(g >= z)
+        def _():
+            slice_up(z, g).start()
+            slice_down(z, g).start()
+
+    @pl.loop(1, 6)
+    def _(k):
+        low, high = up_source(k), down_source(k)
+        rise, fall = rises(low), planes - 1 - rises(high)
+
+        @pl.loop(0, planes)
+        def _(g):
+            @pl.when((g >= low) & (k <= rise))
+            def _():
+                slice_up(low, g).wait_recv()
+
+                @pl.when(k < rise)
+                def _():
+                    slice_up(low, g).start()
+
+            @pl.when((g >= high) & (k <= fall))
+            def _():
+                slice_down(high, g).wait_recv()
+
+                @pl.when(k < fall)
+                def _():
+                    slice_down(high, g).start()
+
+    def shock_step(k):
+        for h in range(2):
+            shock_up(up_source(k), h).wait_recv()
+            shock_down(down_source(k), h).wait_recv()
+            if k < 3 or h == 0:
+                shock_up(up_source(k), h).start()
+            if k < 3 or h == 1:
+                shock_down(down_source(k), h).start()
+
+    shock_step(1)
+
+    acc[...] = jnp.zeros_like(acc)
+    for g in reversed(range(planes)):
+        rows = (g + 1) * width
+
+        def add(q, _):
+            left = slices[q, 0 : g + 1].reshape(rows, height)
+            at = pl.ds(pl.multiple_of(q * height, height), height)
+            acc[0:rows] += jnp.dot(left, loads[at, :], preferred_element_type=jnp.float32)
+            return 0
+
+        lax.fori_loop(g * per_plane, (g + 1) * per_plane, add, 0)
+    full[me, :, :, 0:sets] = acc[:, 0:sets].astype(jnp.bfloat16).reshape(planes, width, sets)
+    basis = acc[:, sets : sets + nb] + acc[:, sets + nb : sets + 2 * nb]
+    high = basis.astype(jnp.bfloat16)
+    low = (basis - high.astype(jnp.float32)).astype(jnp.bfloat16)
+    full[me, :, :, sets : sets + 2 * nb] = jnp.concatenate([high, low], axis=1).reshape(
+        planes, width, 2 * nb
+    )
+
+    core = lax.rem(me, 2)
+    x, y = lax.rem(me // 2, 4), me // 8
+    ia, ib = x + core * (y - x), y + core * (x - y)
+
+    def pid(i, j):
+        return lax.rem(i, 4) * (2 + 6 * core) + lax.rem(j, 4) * (8 - 6 * core) + core
+
+    next_a, last_a = pid(ia + 1, ib), pid(ia + 3, ib)
+    next_b, last_b = pid(ia, ib + 1), pid(ia, ib + 3)
+    partner = me + 1 - 2 * core
+    sent = []
+
+    def piece(q, h):
+        return full.at[q, pl.ds(h * (planes // 2), planes // 2)]
+
+    def give(q, h, to):
+        copy = push(
+            piece(q, h), piece(q, h), g_send.at[len(sent)], g_recv.at[q * 2 + h], {"path": to}
+        )
+        copy.start()
+        sent.append(copy)
+
+    def take(q, h):
+        push(
+            piece(q, h), piece(q, h), g_send.at[0], g_recv.at[q * 2 + h], {"path": partner}
+        ).wait_recv()
+
+    for h in range(2):
+        give(me, h, next_a)
+        give(me, h, last_a)
+        give(me, h, next_b)
+        give(me, h, last_b)
+    for h in range(2):
+        give(me, h, partner)
+    q1, q2, q3 = pid(ia + 3, ib), pid(ia + 1, ib), pid(ia + 2, ib)
+    take(q1, 0)
+    give(q1, 0, next_a)
+    take(q2, 0)
+    take(q1, 1)
+    take(q2, 1)
+    give(q2, 1, last_a)
+    for q in (q1, q2):
+        for h in range(2):
+            give(q, h, next_b)
+            give(q, h, last_b)
+            give(q, h, partner)
+    for h in range(2):
+        take(q3, h)
+        give(q3, h, next_b)
+        give(q3, h, last_b)
+        give(q3, h, partner)
+
+    shock_step(2)
+
+    for i in (ia, ia + 3, ia + 1, ia + 2):
+        r1, r2 = pid(i, ib + 3), pid(i, ib + 1)
+        take(r1, 0)
+        give(r1, 0, next_b)
+        take(r2, 0)
+        take(r1, 1)
+        take(r2, 1)
+        give(r2, 1, last_b)
+        for r in (r1, r2):
+            for h in range(2):
+                give(r, h, partner)
+
+    shock_step(3)
+
+    for i in (ia, ia + 3, ia + 1, ia + 2):
+        r3 = pid(i, ib + 2)
+        for h in range(2):
+            take(r3, h)
+            give(r3, h, partner)
+
+    @pl.loop(0, group // 2)
+    def _(q):
+        for h in range(2):
+            take(2 * q + 1 - core, h)
+
+    shock_up(up_source(4), 0).wait_recv()
+    shock_down(down_source(4), 1).wait_recv()
+
+    acc2 = acc
+    acc2[...] = jnp.zeros_like(acc2)
+
+    def drive(n, _):
+        source = lax.rem(
+            z + planes + jnp.where(lax.rem(n, 2) == 1, -((n + 1) // 2), n // 2), planes
+        )
+        left = shocks[source].reshape(2 * half_rows, cols)
+        right = full[:, source].reshape(cols, full.shape[3])
+        acc2[...] += jnp.dot(left, right, preferred_element_type=jnp.float32)
+        return 0
+
+    lax.fori_loop(0, planes, drive, 0)
+    drive_ref[...] = acc2[:, 0:sets]
+    proj_ref[...] = acc2[:, sets : sets + nb] + acc2[:, sets + nb : sets + 2 * nb]
+
+    for copy in sent:
+        copy.wait_send()
+    for k in range(0, 4):
+        for h in range(2):
+            if k < 3 or h == 0:
+                shock_up(up_source(k), h).wait_send()
+            if k < 3 or h == 1:
+                shock_down(down_source(k), h).wait_send()
+
+    @pl.loop(1, planes)
+    def _(d):
+        vol_copy(d).wait_send()
+
+    @pl.when(me >= per_plane * z)
+    def _():
+        @pl.loop(1, group)
+        def _(d):
+            slice_copy(d).wait_send()
+
+    @pl.loop(0, 5)
+    def _(k):
+        low, high = up_source(k), down_source(k)
+        rise, fall = rises(low), planes - 1 - rises(high)
+
+        @pl.loop(0, planes)
+        def _(g):
+            @pl.when((g >= low) & (k < rise))
+            def _():
+                slice_up(low, g).wait_send()
+
+            @pl.when((g >= high) & (k < fall))
+            def _():
+                slice_down(high, g).wait_send()
+
+
+def front(shocks, chol_factor, factor_vol, trade_loading, basis_loading, steps):
+    planes, group = lax.axis_size("fac"), lax.axis_size("path")
+    rows, cols = shocks.shape
+    height = chol_factor.shape[0]
+    width = cols // group
+    total, sets = trade_loading.shape
+    nb = basis_loading.shape[1]
+    wide = sets + 2 * nb
+    vmem = pl.BlockSpec(memory_space=pltpu.VMEM)
+    hbm = pl.BlockSpec(memory_space=pl.ANY)
+    dma = pltpu.SemaphoreType.DMA
+    return pl.pallas_call(
+        functools.partial(front_kernel, planes, group, 1.0 / math.sqrt(steps)),
+        out_shape=(
+            jax.ShapeDtypeStruct((rows, sets), jnp.float32),
+            jax.ShapeDtypeStruct((rows, nb), jnp.float32),
+        ),
+        in_specs=[vmem, hbm, vmem, hbm, vmem],
+        out_specs=(vmem, vmem),
+        scratch_shapes=[
+            pltpu.VMEM((group, width, height), jnp.bfloat16),
+            pltpu.VMEM((group, planes, width, height), jnp.bfloat16),
+            pltpu.VMEM((planes, 2, rows // 2, cols), jnp.bfloat16),
+            pltpu.VMEM((planes, cols // 128, 128), jnp.float32),
+            pltpu.VMEM((total, wide), jnp.bfloat16),
+            pltpu.VMEM((group, planes, width, wide), jnp.bfloat16),
+            pltpu.VMEM((rows, wide), jnp.float32),
+            dma((3,)),
+            dma((group,)),
+            dma((group,)),
+            dma((planes,)),
+            dma((planes,)),
+            dma((2 * planes,)),
+            dma((2 * planes,)),
+            dma((2 * planes,)),
+            dma((planes * planes,)),
+            dma((planes * planes,)),
+            dma((planes * planes,)),
+            dma((64,)),
+            dma((2 * group,)),
+        ],
+        compiler_params=pltpu.CompilerParams(
+            collective_id=0, has_side_effects=True, vmem_limit_bytes=62 * 2**20
+        ),
+    )(chol_factor, shocks, factor_vol, trade_loading, basis_loading)
+
+
 def on_device(shocks, chol_factor, factor_vol, trade_loading, basis_loading, trade_set):
     step_count, path_count, fac_width = shocks.shape
     row_count = step_count * path_count
-    flat_shocks = shocks.reshape(row_count, fac_width)
-    factor_share = F // lax.axis_size("fac")
-    contract_last = (((1,), (1,)), ((), ()))
-    full_rows = lax.all_gather(chol_factor, "path", axis=0, tiled=True)
-    increments = lax.psum_scatter(
-        lax.dot_general(full_rows, flat_shocks, contract_last, preferred_element_type=jnp.float32),
-        "fac",
-        scatter_dimension=0,
-        tiled=True,
-    )
-    scaled = increments.reshape(factor_share, step_count, path_count) * (
-        factor_vol[:, None, None] / math.sqrt(step_count)
-    )
-    levels = jnp.cumsum(scaled, axis=1).astype(jnp.bfloat16).reshape(factor_share, row_count)
-    basis_count = basis_loading.shape[1]
-    contract_first = (((0,), (0,)), ((), ()))
-    piece = lax.all_gather(levels, "fac", axis=0, tiled=True)
-    trade_sum = lax.dot_general(
-        piece, trade_loading, contract_first, preferred_element_type=jnp.float32
-    )
-    basis_sum = lax.dot_general(
-        piece, basis_loading, contract_first, preferred_element_type=jnp.float32
-    )
     sets_here = NSETS // lax.axis_size("fac")
     local_set = trade_set % sets_here
     member = (local_set[:, None] == jnp.arange(sets_here, dtype=jnp.int32)[None, :]).astype(
         jnp.bfloat16
     )
-    drive = trade_sum.reshape(step_count, path_count, -1)
-    proj = basis_sum.reshape(step_count, path_count, basis_count)
+    drive, proj = front(
+        shocks.reshape(row_count, fac_width),
+        chol_factor,
+        factor_vol.reshape(-1, 128),
+        trade_loading,
+        basis_loading,
+        step_count,
+    )
+    drive = drive.reshape(step_count, path_count, -1)
+    proj = proj.reshape(step_count, path_count, -1)
     return tail(drive, proj, member, path_count * lax.axis_size("path"))
 
 

time: 313 us -> 172 us (0.55)
  the two profiles are of different devices: /device:TPU:1 before, /device:TPU:33 now
where the time goes in v2:
time: 172 us
  Pallas kernels  166 us (97%)
  local copies, waits for them, and re-layouts  4.65 us (3%)
    pallas_call x1, Pallas kernels, front(): pl.pallas_call(functools.partial(front_kernel, planes, group, 1.0 / math....  118 us
    pallas_call x1, Pallas kernels, tail(): pl.pallas_call(functools.partial(tail_kernel, group, total_paths), out_sh...  48.5 us
    unnamed x4, local copies, waits for them, and re-layouts  4.65 us

profile of v2, /device:TPU:33, one launch (start us, length us, event | category | flops | bytes accessed | tf_op | source)
XLA Modules:
  0.0 171.9 jit_solution(9608240000936135125)
XLA Ops:
  0.0 0.0 copy-start
  0.0 2.8 %copy.7.basis_ref = bf16[8192,64]{1,0:T(8,128)(2,1)} copy(bf16[8192,64]{0,1:T(8,128)(2,1)} %param.10) | data formatting | bytes 2097152 | tf_op args[4]
  2.8 117.7 %shard_map.64 = (f32[256,512]{1,0:T(8,128)}, f32[256,64]{1,0:T(8,128)}) custom-call(bf16[256,1024]{1,0:T(8,128)(2,1)} %chol_ref.1, bf16[256,1024]{1,0:T(8,128)(2,1)} %bitcast.5, f32[8,128]{1,0:T(8,128)} %bitcast.7, bf16[8192,512]{1,0:T(8,128)(2,1)} %trade_hbm.1, bf16[8192,64]{1,0:T(8,128)(2,1)} %copy.7.basis_ref), custom_call_target="tpu_custom_call" | custom-call | tf_op jit(solution)/shard_map/pallas_call | solution.py:553
  120.5 0.0 copy-done
  120.6 0.9 fusion.member_ref
  121.5 48.5 %shard_map.65 = f32[4,64,512]{2,1,0:T(8,128)} custom-call(f32[4,64,512]{2,1,0:T(8,128)} %bitcast.4, f32[4,64,64]{2,1,0:T(8,128)} %bitcast.6, bf16[512,512]{1,0:T(8,128)(2,1)} %fusion.member_ref), custom_call_target="tpu_custom_call" | custom-call | tf_op jit(solution)/shard_map/pallas_call | solution.py:172
  170.0 1.9 %copy.9 = f32[4,64,512]{2,1,0:T(8,128)} copy(f32[4,64,512]{2,1,0:T(8,128)} %shard_map.65) | data formatting | bytes 1048576
  (1 shorter events, 0.0 us)
Async XLA Ops:
  0.0 120.5 %copy-start = (s32[512]{0:T(512)S(1)}, s32[512]{0:T(512)}, u32[]{:S(2)}) copy-start(s32[512]{0:T(512)} %param.11) | copy-start | bytes 6148

commit v3 on v2

v3 whole, which is shorter than its diff:
```python
import functools
import math

import jax
import jax.numpy as jnp
from jax import lax
from jax.experimental import pallas as pl
from jax.experimental.pallas import tpu as pltpu
from jax.sharding import PartitionSpec as P

NSETS = 4096
MESH = pl.DeviceIdType.MESH
HIGH = lax.Precision.HIGHEST


def split_dot(a, b):
    high = a.astype(jnp.bfloat16)
    low = (a - high.astype(jnp.float32)).astype(jnp.bfloat16)
    both = jnp.dot(
        jnp.concatenate([high, low], axis=0), b, preferred_element_type=jnp.float32
    )
    rows = a.shape[0]
    return both[:rows] + both[rows:]


def invert(mats):
    n = mats[0].shape[0]
    count = len(mats)
    row = lax.broadcasted_iota(jnp.int32, (n, 2 * n), 0)
    lane = lax.broadcasted_iota(jnp.int32, (n, 2 * n), 1)
    eye = jnp.where(lane == row + n, 1.0, 0.0)
    wide = [jnp.concatenate([m, jnp.zeros_like(m)], axis=1) + eye for m in mats]
    blocks = tuple(tuple(w[8 * b : 8 * b + 8] for b in range(n // 8)) for w in wide)
    sub = lax.broadcasted_iota(jnp.int32, (8, 1), 0)

    def body(_, blocks):
        done = []
        for m in range(count):
            rows = list(blocks[m])
            for k in range(8):
                pivot_row = rows[0][k : k + 1, :]
                inverse = 1.0 / pivot_row[:, k : k + 1]
                scaled = pivot_row * inverse
                fresh = []
                for b in range(n // 8):
                    col = rows[b][:, k : k + 1]
                    if b == 0:
                        col = jnp.where(sub == k, col - 1.0, col)
                    fresh.append(rows[b] - col * scaled)
                rows = fresh
            rows = rows[1:] + rows[:1]
            done.append(tuple(pltpu.roll(r, 2 * n - 8, 1) for r in rows))
        return tuple(done)

    blocks = lax.fori_loop(0, n // 8, body, blocks)
    return [jnp.concatenate(b, axis=0)[:, :n] for b in blocks]


def push(src, dst, send_sem, recv_sem, where):
    return pltpu.make_async_remote_copy(
        src_ref=src, dst_ref=dst, send_sem=send_sem, recv_sem=recv_sem,
        device_id=where, device_id_type=MESH,
    )


def rises(s):
    extra = [0, 1, 3, 3, 0, 1, 1, 0]
    total = 2
    for at, more in enumerate(extra):
        if more:
            total = total + jnp.where(s == at, more, 0)
    return total


def kernel(
    planes, group, scale, total_paths,
    chol_ref, shock_hbm, vol_ref, trade_hbm, basis_ref, member_ref, out_ref,
    turned, slices, shocks, vols, loads, full, acc,
    gram_part, gram_in, gram_sum, part, landed, total, base,
    local_sem, a_send, a_recv, v_send, v_recv, s_up, s_down, s_recv,
    c_up, c_down, c_recv, g_send, g_recv, t_send, t_recv,
):
    me = lax.axis_index("path")
    z = lax.axis_index("fac")
    above, below = {"fac": lax.rem(z + 1, planes)}, {"fac": lax.rem(z + planes - 1, planes)}
    per_plane = group // planes
    height, cols = chol_ref.shape
    width = cols // group
    sets = trade_hbm.shape[1]
    nb = basis_ref.shape[0]
    half_rows = shock_hbm.shape[0] // 2
    steps, paths = out_ref.shape[0:2]

    barrier = pltpu.get_barrier_semaphore()

    @pl.loop(1, group)
    def _(d):
        pl.semaphore_signal(
            barrier, inc=1, device_id={"path": lax.rem(me + d, group)}, device_id_type=MESH
        )

    @pl.loop(1, planes)
    def _(d):
        pl.semaphore_signal(
            barrier, inc=1, device_id={"fac": lax.rem(z + d, planes)}, device_id_type=MESH
        )

    load_shocks = [
        pltpu.make_async_copy(
            shock_hbm.at[pl.ds(h * half_rows, half_rows)], shocks.at[z, h], local_sem.at[1 + h]
        )
        for h in range(2)
    ]
    for copy in load_shocks:
        copy.start()
    load_trades = pltpu.make_async_copy(trade_hbm, loads.at[:, 0:sets], local_sem.at[0])
    load_trades.start()

    for b in range(cols // 128):
        block = chol_ref[:, 128 * b : 128 * (b + 1)].T
        at = pl.ds(b * (128 // width), 128 // width)
        turned[at] = block.reshape(128 // width, width, height)
    vols[z] = vol_ref[...]
    for g in range(planes - 1):
        slices[g * per_plane : (g + 1) * per_plane, g + 1 : planes] = jnp.zeros(
            (per_plane, planes - 1 - g, width, height), jnp.bfloat16
        )
    for copy in load_shocks:
        copy.wait()

    pl.semaphore_wait(barrier, group - 1 + planes - 1)

    def up_source(k):
        return lax.rem(z + planes - k, planes)

    def down_source(k):
        return lax.rem(z + k, planes)

    def slice_copy(d):
        to = lax.rem(me + d, group)
        return push(turned.at[to], slices.at[me, z], a_send.at[to], a_recv.at[me], {"path": to})

    def slice_taken(source):
        return push(
            turned.at[source], slices.at[source, z], a_send.at[source], a_recv.at[source],
            {"path": source},
        )

    @pl.when(me >= per_plane * z)
    def _():
        @pl.loop(1, group)
        def _(d):
            slice_copy(d).start()

        slices[me, z] = turned[me]

    def shock_up(s, h):
        return push(shocks.at[s, h], shocks.at[s, h], s_up.at[s * 2 + h], s_recv.at[s * 2 + h], above)

    def shock_down(s, h):
        return push(
            shocks.at[s, h], shocks.at[s, h], s_down.at[s * 2 + h], s_recv.at[s * 2 + h], below
        )

    def vol_copy(d):
        to = lax.rem(z + d, planes)
        return push(vols.at[z], vols.at[z], v_send.at[to], v_recv.at[z], {"fac": to})

    def vol_taken(d):
        source = lax.rem(z + d, planes)
        return push(
            vols.at[source], vols.at[source], v_send.at[source], v_recv.at[source], {"fac": source}
        )

    @pl.loop(1, planes)
    def _(d):
        vol_copy(d).start()

    shock_up(z, 0).start()
    shock_down(z, 0).start()

    @pl.loop(1, group)
    def _(d):
        source = lax.rem(me + d, group)

        @pl.when(source >= per_plane * z)
        def _():
            slice_taken(source).wait_recv()

    def block(s, g):
        return slices.at[pl.ds(g * per_plane, per_plane), s]

    def slice_up(s, g):
        return push(
            block(s, g), block(s, g), c_up.at[s * planes + g], c_recv.at[s * planes + g], above
        )

    def slice_down(s, g):
        return push(
            block(s, g), block(s, g), c_down.at[s * planes + g], c_recv.at[s * planes + g], below
        )

    @pl.loop(0, planes)
    def _(g):
        @pl.when(g >= z)
        def _():
            slice_up(z, g).start()
            slice_down(z, g).start()

    shock_up(z, 1).start()
    shock_down(z, 1).start()

    @pl.loop(1, planes)
    def _(d):
        vol_taken(d).wait_recv()

    load_trades.wait()
    vol_rows = vols[...].reshape(planes * vol_ref.shape[0], 128) * scale
    vol_rows = jnp.concatenate(
        [vol_rows, jnp.zeros((128 - vol_rows.shape[0], 128), jnp.float32)], axis=0
    )

    def scale_rows(c, columns):
        column = columns[:, 0:1]
        at = pl.ds(pl.multiple_of(c * 128, 128), 128)
        loads[at, 0:sets] = (loads[at, 0:sets].astype(jnp.float32) * column).astype(jnp.bfloat16)
        basis = basis_ref[:, at].astype(jnp.float32).T * column
        high = basis.astype(jnp.bfloat16)
        low = (basis - high.astype(jnp.float32)).astype(jnp.bfloat16)
        loads[at, sets : sets + 2 * nb] = jnp.concatenate([high, low], axis=1)
        return pltpu.roll(columns, 127, 1)

    lax.fori_loop(0, loads.shape[0] // 128, scale_rows, vol_rows.T)

    def slice_step(k):
        low, high = up_source(k), down_source(k)
        rise, fall = rises(low), planes - 1 - rises(high)

        @pl.loop(0, planes)
        def _(g):
            @pl.when((g >= low) & (k <= rise))
            def _():
                slice_up(low, g).wait_recv()

                @pl.when(k < rise)
                def _():
                    slice_up(low, g).start()

            @pl.when((g >= high) & (k <= fall))
            def _():
                slice_down(high, g).wait_recv()

                @pl.when(k < fall)
                def _():
                    slice_down(high, g).start()

    def shock_step(k):
        for h in range(2):
            shock_up(up_source(k), h).wait_recv()
            shock_down(down_source(k), h).wait_recv()
            if k < 3 or h == 0:
                shock_up(up_source(k), h).start()
            if k < 3 or h == 1:
                shock_down(down_source(k), h).start()

    offsets = [0, -1, 1, -2, 2, -3, 3, 4]

    def plane_at(n):
        return lax.rem(z + planes + offsets[n], planes)

    waves = [(0, 5), (5, 8)]
    cuts = [(0, 3), (3, 5), (5, 6), (6, 8)]

    def make(first, last):
        count = (last - first) * width
        acc[0:count] = jnp.zeros((count, acc.shape[1]), jnp.float32)

        def add(q, _):
            left = jnp.concatenate(
                [slices[q, plane_at(n)] for n in range(first, last)], axis=0
            )
            at = pl.ds(pl.multiple_of(q * height, height), height)
            acc[0:count] += jnp.dot(left, loads[at, :], preferred_element_type=jnp.float32)
            return 0

        lax.fori_loop(0, group, add, 0)
        full[me, first:last, :, 0:sets] = (
            acc[0:count, 0:sets].astype(jnp.bfloat16).reshape(last - first, width, sets)
        )
        basis = acc[0:count, sets : sets + nb] + acc[0:count, sets + nb : sets + 2 * nb]
        high = basis.astype(jnp.bfloat16)
        low = (basis - high.astype(jnp.float32)).astype(jnp.bfloat16)
        full[me, first:last, :, sets : sets + 2 * nb] = jnp.concatenate(
            [high, low], axis=1
        ).reshape(last - first, width, 2 * nb)

    core = lax.rem(me, 2)
    x, y = lax.rem(me // 2, 4), me // 8
    ia, ib = x + core * (y - x), y + core * (x - y)

    def pid(i, j):
        return lax.rem(i, 4) * (2 + 6 * core) + lax.rem(j, 4) * (8 - 6 * core) + core

    next_a, last_a = pid(ia + 1, ib), pid(ia + 3, ib)
    next_b, last_b = pid(ia, ib + 1), pid(ia, ib + 3)
    partner = me + 1 - 2 * core
    q1, q2, q3 = pid(ia + 3, ib), pid(ia + 1, ib), pid(ia + 2, ib)
    sent = []

    def piece(q, cut):
        first, last = cuts[cut]
        return full.at[q, pl.ds(first, last - first)]

    def give(q, cut, to):
        copy = push(
            piece(q, cut), piece(q, cut), g_send.at[len(sent)], g_recv.at[q * 4 + cut], {"path": to}
        )
        copy.start()
        sent.append(copy)

    def take(q, cut):
        push(
            piece(q, cut), piece(q, cut), g_send.at[0], g_recv.at[q * 4 + cut], {"path": partner}
        ).wait_recv()

    def gather_own(w):
        for cut in (2 * w, 2 * w + 1):
            give(me, cut, next_a)
            give(me, cut, last_a)
            give(me, cut, next_b)
            give(me, cut, last_b)
        for cut in (2 * w, 2 * w + 1):
            give(me, cut, partner)

    def gather_first(w):
        up, down = 2 * w, 2 * w + 1
        take(q1, up)
        give(q1, up, next_a)
        take(q2, down)
        give(q2, down, last_a)
        take(q1, down)
        take(q2, up)
        for q in (q1, q2):
            for cut in (up, down):
                give(q, cut, next_b)
                give(q, cut, last_b)
                give(q, cut, partner)
        for cut in (up, down):
            take(q3, cut)
            give(q3, cut, next_b)
            give(q3, cut, last_b)
            give(q3, cut, partner)

    def gather_second(w):
        up, down = 2 * w, 2 * w + 1
        for i in (ia, ia + 3, ia + 1, ia + 2):
            r1, r2 = pid(i, ib + 3), pid(i, ib + 1)
            take(r1, up)
            give(r1, up, next_b)
            take(r2, down)
            give(r2, down, last_b)
            take(r1, down)
            take(r2, up)
            for r in (r1, r2):
                for cut in (up, down):
                    give(r, cut, partner)

    def gather_last(w):
        for i in (ia, ia + 3, ia + 1, ia + 2):
            r3 = pid(i, ib + 2)
            for cut in (2 * w, 2 * w + 1):
                take(r3, cut)
                give(r3, cut, partner)

    def gather_partner(w):
        @pl.loop(0, group // 2)
        def _(q):
            for cut in (2 * w, 2 * w + 1):
                take(2 * q + 1 - core, cut)

    slice_step(1)
    slice_step(2)
    make(*waves[0])
    gather_own(0)
    slice_step(3)
    gather_first(0)
    slice_step(4)
    shock_step(1)
    gather_second(0)
    slice_step(5)
    make(*waves[1])
    gather_own(1)
    gather_last(0)
    gather_first(1)
    shock_step(2)
    gather_second(1)
    gather_partner(0)
    shock_step(3)

    acc[...] = jnp.zeros_like(acc)

    def drive(first, last):
        for n in range(first, last):
            left = shocks[plane_at(n)].reshape(2 * half_rows, cols)
            right = full[:, n].reshape(cols, full.shape[3])
            acc[...] += jnp.dot(left, right, preferred_element_type=jnp.float32)

    drive(0, 5)
    gather_last(1)
    gather_partner(1)
    shock_up(up_source(4), 0).wait_recv()
    shock_down(down_source(4), 1).wait_recv()
    drive(5, 8)

    def scatter(src, dst, lane, d):
        to = lax.rem(me + d, group)
        return push(
            src.at[to], dst.at[me], t_send.at[lane * group + to], t_recv.at[lane * group + me],
            {"path": to},
        )

    def share(src, lane, d):
        to = lax.rem(me + d, group)
        return push(
            src.at[me], src.at[me], t_send.at[lane * group + to], t_recv.at[lane * group + me],
            {"path": to},
        )

    def taken(dst, lane, d):
        source = lax.rem(me + d, group)
        return push(
            dst.at[source], dst.at[source], t_send.at[lane * group + source],
            t_recv.at[lane * group + source], {"path": source},
        )

    def each(action):
        @pl.loop(1, group)
        def _(d):
            action(d)

    contract = (((0,), (0,)), ((), ()))
    rows = nb // 8
    w = jnp.zeros((paths, nb), jnp.float32)
    for t in range(steps):
        here = pl.ds(t * paths, paths)
        w = w + (acc[here, sets : sets + nb] + acc[here, sets + nb : sets + 2 * nb])
        basis = jnp.tanh(w)
        base[t] = basis
        gram = lax.dot_general(
            basis, basis, contract, precision=HIGH, preferred_element_type=jnp.float32
        )
        gram = jnp.concatenate([gram, jnp.zeros_like(gram)], axis=1)
        gram_part[t * rows : (t + 1) * rows] = gram.reshape(rows, 8, 2 * nb)
    each(lambda d: scatter(gram_part, gram_in, 0, d).start())
    gram_in[me] = gram_part[me]

    v = jnp.zeros((paths, sets), jnp.float32)
    for t in range(steps):
        v = v + acc[pl.ds(t * paths, paths), 0:sets]
        values = jnp.maximum(v, 0.0) + jnp.log(1.0 + jnp.exp(-jnp.abs(v))) - 1.0
        moment = lax.dot_general(
            base[t], values, contract, precision=HIGH, preferred_element_type=jnp.float32
        )
        part[t * rows : (t + 1) * rows] = moment.reshape(rows, 8, sets)
    each(lambda d: scatter(part, landed, 1, d).start())
    landed[me] = part[me]

    each(lambda d: taken(gram_in, 0, d).wait_recv())
    gram_sum[me] = jnp.sum(gram_in[...], axis=0)
    each(lambda d: share(gram_sum, 2, d).start())

    each(lambda d: taken(landed, 1, d).wait_recv())
    total[me] = split_dot(jnp.sum(landed[...], axis=0), member_ref[...])
    each(lambda d: share(total, 3, d).start())

    each(lambda d: taken(gram_sum, 2, d).wait_recv())
    row = lax.broadcasted_iota(jnp.int32, (nb, nb), 0)
    lane = lax.broadcasted_iota(jnp.int32, (nb, nb), 1)
    ridge = jnp.where(row == lane, 0.01 * total_paths, 0.0)
    inverses = invert(
        [
            gram_sum[t * rows : (t + 1) * rows, :, 0:nb].reshape(nb, nb) + ridge
            for t in range(steps)
        ]
    )
    weights = [
        jnp.dot(base[t], inverses[t], precision=HIGH, preferred_element_type=jnp.float32)
        for t in range(steps)
    ]
    each(lambda d: taken(total, 3, d).wait_recv())
    for t in range(steps):
        moment = total[t * rows : (t + 1) * rows].reshape(nb, sets)
        predicted = jnp.dot(
            weights[t], moment, precision=HIGH, preferred_element_type=jnp.float32
        )
        out_ref[t] = jnp.maximum(predicted, 0.0)

    each(lambda d: scatter(gram_part, gram_in, 0, d).wait_send())
    each(lambda d: scatter(part, landed, 1, d).wait_send())
    each(lambda d: share(gram_sum, 2, d).wait_send())
    each(lambda d: share(total, 3, d).wait_send())
    for copy in sent:
        copy.wait_send()
    for k in range(0, 4):
        for h in range(2):
            if k < 3 or h == 0:
                shock_up(up_source(k), h).wait_send()
            if k < 3 or h == 1:
                shock_down(down_source(k), h).wait_send()

    @pl.loop(1, planes)
    def _(d):
        vol_copy(d).wait_send()

    @pl.when(me >= per_plane * z)
    def _():
        each(lambda d: slice_copy(d).wait_send())

    @pl.loop(0, 5)
    def _(k):
        low, high = up_source(k), down_source(k)
        rise, fall = rises(low), planes - 1 - rises(high)

        @pl.loop(0, planes)
        def _(g):
            @pl.when((g >= low) & (k < rise))
            def _():
                slice_up(low, g).wait_send()

            @pl.when((g >= high) & (k < fall))
            def _():
                slice_down(high, g).wait_send()


def on_device(shocks, chol_factor, factor_vol, trade_loading, basis_loading, trade_set):
    steps, paths, cols = shocks.shape
    planes, group = lax.axis_size("fac"), lax.axis_size("path")
    rows = steps * paths
    height = chol_factor.shape[0]
    width = cols // group
    total, sets = trade_loading.shape
    nb = basis_loading.shape[1]
    wide = sets + 2 * nb
    local_set = trade_set % (NSETS // planes)
    member = (local_set[:, None] == jnp.arange(sets, dtype=jnp.int32)[None, :]).astype(
        jnp.bfloat16
    )
    vmem = pl.BlockSpec(memory_space=pltpu.VMEM)
    hbm = pl.BlockSpec(memory_space=pl.ANY)
    dma = pltpu.SemaphoreType.DMA
    return pl.pallas_call(
        functools.partial(
            kernel, planes, group, 1.0 / math.sqrt(steps), paths * group
        ),
        out_shape=jax.ShapeDtypeStruct((steps, paths, sets), jnp.float32),
        in_specs=[vmem, hbm, vmem, hbm, vmem, vmem],
        out_specs=vmem,
        scratch_shapes=[
            pltpu.VMEM((group, width, height), jnp.bfloat16),
            pltpu.VMEM((group, planes, width, height), jnp.bfloat16),
            pltpu.VMEM((planes, 2, rows // 2, cols), jnp.bfloat16),
            pltpu.VMEM((planes, cols // 128, 128), jnp.float32),
            pltpu.VMEM((total, wide), jnp.bfloat16),
            pltpu.VMEM((group, planes, width, wide), jnp.bfloat16),
            pltpu.VMEM((rows, wide), jnp.float32),
            pltpu.VMEM((group, 8, 2 * nb), jnp.float32),
            pltpu.VMEM((group, 8, 2 * nb), jnp.float32),
            pltpu.VMEM((group, 8, 2 * nb), jnp.float32),
            pltpu.VMEM((group, 8, sets), jnp.float32),
            pltpu.VMEM((group, 8, sets), jnp.float32),
            pltpu.VMEM((group, 8, sets), jnp.float32),
            pltpu.VMEM((steps, paths, nb), jnp.float32),
            dma((3,)),
            dma((group,)),
            dma((group,)),
            dma((planes,)),
            dma((planes,)),
            dma((2 * planes,)),
            dma((2 * planes,)),
            dma((2 * planes,)),
            dma((planes * planes,)),
            dma((planes * planes,)),
            dma((planes * planes,)),
            dma((128,)),
            dma((4 * group,)),
            dma((4 * group,)),
            dma((4 * group,)),
        ],
        compiler_params=pltpu.CompilerParams(
            collective_id=0, has_side_effects=True, vmem_limit_bytes=62 * 2**20
        ),
    )(
        chol_factor,
        shocks.reshape(rows, cols),
        factor_vol.reshape(-1, 128),
        trade_loading,
        basis_loading.T,
        member,
    )


def solution(mesh):
    in_specs = (P(None, "path", "fac"), P("path", "fac"), P("fac"), P(None, "fac"), P(), P("fac"))
    out_specs = P(None, "path", "fac")
    return jax.shard_map(
        on_device, mesh=mesh, in_specs=in_specs, out_specs=out_specs, check_vma=False
    )
```

time: 172 us -> 145 us (0.84)
  the two profiles are of different devices: /device:TPU:33 before, /device:TPU:1 now
where the time goes in v3:
time: 145 us; the launch traced here: 144 us
  Pallas kernels  141 us (97%)
  local copies, waits for them, and re-layouts  1.87 us (1%)
  other arithmetic  1.64 us (1%)
    pallas_call x1, Pallas kernels, on_device(): pl.pallas_call(functools.partial(kernel, planes, group, 1.0 / math.sqrt(s...  141 us

profile of v3, /device:TPU:1, one launch (start us, length us, event | category | flops | bytes accessed | tf_op | source)
XLA Modules:
  0.0 144.5 jit_solution(6161424480771433429)
XLA Ops:
  0.0 0.7 add_select_fusion
  0.7 0.9 fusion.member_ref
  1.6 140.9 %shard_map.64 = f32[4,64,512]{2,1,0:T(8,128)} custom-call(bf16[256,1024]{1,0:T(8,128)(2,1)} %chol_ref.1, bf16[256,1024]{1,0:T(8,128)(2,1)} %bitcast.4, f32[8,128]{1,0:T(8,128)} %bitcast.5, bf16[8192,512]{1,0:T(8,128)(2,1)} %trade_hbm.1, bf16[64,8192]{1,0:T(8,128)(2,1)} %bitcast.3, bf16[512,512]{1,0:T(8,128)(2,1)} %fusion.member_ref), custom_call_target="tpu_custom_call" | custom-call | tf_op jit(solution)/shard_map/pallas_call | solution.py:551
  142.6 1.9 %copy.8 = f32[4,64,512]{2,1,0:T(8,128)} copy(f32[4,64,512]{2,1,0:T(8,128)} %shard_map.64) | data formatting | bytes 1048576

commit v4 on v3

--- a/solution.py
+++ b/solution.py
@@ -8,7 +8,6 @@
 from jax.experimental.pallas import tpu as pltpu
 from jax.sharding import PartitionSpec as P
 
-NSETS = 4096
 MESH = pl.DeviceIdType.MESH
 HIGH = lax.Precision.HIGHEST
 
@@ -16,8 +15,11 @@
 def split_dot(a, b):
     high = a.astype(jnp.bfloat16)
     low = (a - high.astype(jnp.float32)).astype(jnp.bfloat16)
-    both = jnp.dot(
-        jnp.concatenate([high, low], axis=0), b, preferred_element_type=jnp.float32
+    both = lax.dot_general(
+        jnp.concatenate([high, low], axis=0),
+        b,
+        (((1,), (1,)), ((), ())),
+        preferred_element_type=jnp.float32,
     )
     rows = a.shape[0]
     return both[:rows] + both[rows:]
@@ -64,17 +66,13 @@
 
 
 def rises(s):
-    extra = [0, 1, 3, 3, 0, 1, 1, 0]
-    total = 2
-    for at, more in enumerate(extra):
-        if more:
-            total = total + jnp.where(s == at, more, 0)
-    return total
+    return 3 + jnp.where((s >= 2) & (s <= 4), 1, 0)
 
 
 def kernel(
     planes, group, scale, total_paths,
-    chol_ref, shock_hbm, vol_ref, trade_hbm, basis_ref, member_ref, out_ref,
+    chol_hbm, shock_hbm, vol_ref, trade_hbm, basis_hbm, set_ref, out_ref,
+    chol_ref, basis_ref,
     turned, slices, shocks, vols, loads, full, acc,
     gram_part, gram_in, gram_sum, part, landed, total, base,
     local_sem, a_send, a_recv, v_send, v_recv, s_up, s_down, s_recv,
@@ -113,8 +111,13 @@
     ]
     for copy in load_shocks:
         copy.start()
+    load_chol = pltpu.make_async_copy(chol_hbm, chol_ref, local_sem.at[3])
+    load_chol.start()
+    load_basis = pltpu.make_async_copy(basis_hbm, basis_ref, local_sem.at[4])
+    load_basis.start()
     load_trades = pltpu.make_async_copy(trade_hbm, loads.at[:, 0:sets], local_sem.at[0])
     load_trades.start()
+    load_chol.wait()
 
     for b in range(cols // 128):
         block = chol_ref[:, 128 * b : 128 * (b + 1)].T
@@ -207,14 +210,12 @@
             slice_up(z, g).start()
             slice_down(z, g).start()
 
-    shock_up(z, 1).start()
-    shock_down(z, 1).start()
-
     @pl.loop(1, planes)
     def _(d):
         vol_taken(d).wait_recv()
 
     load_trades.wait()
+    load_basis.wait()
     vol_rows = vols[...].reshape(planes * vol_ref.shape[0], 128) * scale
     vol_rows = jnp.concatenate(
         [vol_rows, jnp.zeros((128 - vol_rows.shape[0], 128), jnp.float32)], axis=0
@@ -230,38 +231,38 @@
         loads[at, sets : sets + 2 * nb] = jnp.concatenate([high, low], axis=1)
         return pltpu.roll(columns, 127, 1)
 
-    lax.fori_loop(0, loads.shape[0] // 128, scale_rows, vol_rows.T)
-
-    def slice_step(k):
+    def slice_unit(k, g):
         low, high = up_source(k), down_source(k)
         rise, fall = rises(low), planes - 1 - rises(high)
 
+        @pl.when((g >= low) & (k <= rise))
+        def _():
+            slice_up(low, g).wait_recv()
+
+            @pl.when(k < rise)
+            def _():
+                slice_up(low, g).start()
+
+        @pl.when((g >= high) & (k <= fall))
+        def _():
+            slice_down(high, g).wait_recv()
+
+            @pl.when(k < fall)
+            def _():
+                slice_down(high, g).start()
+
+    def slice_step(k):
         @pl.loop(0, planes)
         def _(g):
-            @pl.when((g >= low) & (k <= rise))
-            def _():
-                slice_up(low, g).wait_recv()
-
-                @pl.when(k < rise)
-                def _():
-                    slice_up(low, g).start()
-
-            @pl.when((g >= high) & (k <= fall))
-            def _():
-                slice_down(high, g).wait_recv()
-
-                @pl.when(k < fall)
-                def _():
-                    slice_down(high, g).start()
-
-    def shock_step(k):
-        for h in range(2):
-            shock_up(up_source(k), h).wait_recv()
-            shock_down(down_source(k), h).wait_recv()
-            if k < 3 or h == 0:
-                shock_up(up_source(k), h).start()
-            if k < 3 or h == 1:
-                shock_down(down_source(k), h).start()
+            slice_unit(k, g)
+
+    def shock_step(k, h):
+        shock_up(up_source(k), h).wait_recv()
+        shock_down(down_source(k), h).wait_recv()
+        if k < 3 or h == 0:
+            shock_up(up_source(k), h).start()
+        if k < 3 or h == 1:
+            shock_down(down_source(k), h).start()
 
     offsets = [0, -1, 1, -2, 2, -3, 3, 4]
 
@@ -271,19 +272,27 @@
     waves = [(0, 5), (5, 8)]
     cuts = [(0, 3), (3, 5), (5, 6), (6, 8)]
 
-    def make(first, last):
+    def make(first, last, k):
         count = (last - first) * width
         acc[0:count] = jnp.zeros((count, acc.shape[1]), jnp.float32)
 
-        def add(q, _):
+        @pl.loop(0, planes)
+        def _(g):
             left = jnp.concatenate(
-                [slices[q, plane_at(n)] for n in range(first, last)], axis=0
+                [
+                    jnp.concatenate(
+                        [slices[g * per_plane + r, plane_at(n)] for n in range(first, last)], axis=0
+                    )
+                    for r in range(per_plane)
+                ],
+                axis=1,
             )
-            at = pl.ds(pl.multiple_of(q * height, height), height)
+            deep = height * per_plane
+            at = pl.ds(pl.multiple_of(g * deep, deep), deep)
             acc[0:count] += jnp.dot(left, loads[at, :], preferred_element_type=jnp.float32)
-            return 0
-
-        lax.fori_loop(0, group, add, 0)
+            if k:
+                slice_unit(k, g)
+
         full[me, first:last, :, 0:sets] = (
             acc[0:count, 0:sets].astype(jnp.bfloat16).reshape(last - first, width, sets)
         )
@@ -378,24 +387,33 @@
             for cut in (2 * w, 2 * w + 1):
                 take(2 * q + 1 - core, cut)
 
-    slice_step(1)
+    def scale_part(g, columns):
+        columns = lax.fori_loop(g * per_part, (g + 1) * per_part, scale_rows, columns)
+        slice_unit(1, g)
+        return columns
+
+    per_part = loads.shape[0] // 128 // planes
+    lax.fori_loop(0, planes, scale_part, vol_rows.T)
+    shock_up(z, 1).start()
+    shock_down(z, 1).start()
     slice_step(2)
-    make(*waves[0])
+    shock_step(1, 0)
+    make(*waves[0], 3)
     gather_own(0)
-    slice_step(3)
+    shock_step(1, 1)
+    slice_step(4)
     gather_first(0)
-    slice_step(4)
-    shock_step(1)
+    shock_step(2, 0)
+    make(*waves[1], 0)
+    gather_own(1)
     gather_second(0)
-    slice_step(5)
-    make(*waves[1])
-    gather_own(1)
+    shock_step(2, 1)
+    gather_first(1)
     gather_last(0)
-    gather_first(1)
-    shock_step(2)
+    shock_step(3, 0)
+    shock_step(3, 1)
     gather_second(1)
     gather_partner(0)
-    shock_step(3)
 
     acc[...] = jnp.zeros_like(acc)
 
@@ -470,7 +488,10 @@
     each(lambda d: share(gram_sum, 2, d).start())
 
     each(lambda d: taken(landed, 1, d).wait_recv())
-    total[me] = split_dot(jnp.sum(landed[...], axis=0), member_ref[...])
+    member = (
+        lax.broadcasted_iota(jnp.int32, (sets, set_ref.shape[1]), 0) == lax.rem(set_ref[...], sets)
+    ).astype(jnp.float32).astype(jnp.bfloat16)
+    total[me] = split_dot(jnp.sum(landed[...], axis=0), member)
     each(lambda d: share(total, 3, d).start())
 
     each(lambda d: taken(gram_sum, 2, d).wait_recv())
@@ -516,7 +537,7 @@
     def _():
         each(lambda d: slice_copy(d).wait_send())
 
-    @pl.loop(0, 5)
+    @pl.loop(0, 4)
     def _(k):
         low, high = up_source(k), down_source(k)
         rise, fall = rises(low), planes - 1 - rises(high)
@@ -541,10 +562,6 @@
     total, sets = trade_loading.shape
     nb = basis_loading.shape[1]
     wide = sets + 2 * nb
-    local_set = trade_set % (NSETS // planes)
-    member = (local_set[:, None] == jnp.arange(sets, dtype=jnp.int32)[None, :]).astype(
-        jnp.bfloat16
-    )
     vmem = pl.BlockSpec(memory_space=pltpu.VMEM)
     hbm = pl.BlockSpec(memory_space=pl.ANY)
     dma = pltpu.SemaphoreType.DMA
@@ -553,9 +570,11 @@
             kernel, planes, group, 1.0 / math.sqrt(steps), paths * group
         ),
         out_shape=jax.ShapeDtypeStruct((steps, paths, sets), jnp.float32),
-        in_specs=[vmem, hbm, vmem, hbm, vmem, vmem],
+        in_specs=[hbm, hbm, vmem, hbm, hbm, vmem],
         out_specs=vmem,
         scratch_shapes=[
+            pltpu.VMEM(chol_factor.shape, jnp.bfloat16),
+            pltpu.VMEM((nb, total), jnp.bfloat16),
             pltpu.VMEM((group, width, height), jnp.bfloat16),
             pltpu.VMEM((group, planes, width, height), jnp.bfloat16),
             pltpu.VMEM((planes, 2, rows // 2, cols), jnp.bfloat16),
@@ -570,7 +589,7 @@
             pltpu.VMEM((group, 8, sets), jnp.float32),
             pltpu.VMEM((group, 8, sets), jnp.float32),
             pltpu.VMEM((steps, paths, nb), jnp.float32),
-            dma((3,)),
+            dma((5,)),
             dma((group,)),
             dma((group,)),
             dma((planes,)),
@@ -595,7 +614,7 @@
         factor_vol.reshape(-1, 128),
         trade_loading,
         basis_loading.T,
-        member,
+        trade_set.reshape(1, -1),
     )
 
 

time: 145 us -> 125 us (0.86)
  Pallas kernels: 141 us -> 122 us
  other arithmetic: 1.64 us -> 0 us
    pallas_call x1, Pallas kernels: 141 us -> 122 us  [on_device(): pl.pallas_call(functools.partial(kernel, planes, group, 1.0 / math.sqrt(s...]
where the time goes in v4:
time: 125 us; the launch traced here: 124 us
  Pallas kernels  122 us (98%)
  local copies, waits for them, and re-layouts  1.87 us (1%)
    pallas_call x1, Pallas kernels, on_device(): pl.pallas_call(functools.partial(kernel, planes, group, 1.0 / math.sqrt(s...  122 us

profile of v4, /device:TPU:1, one launch (start us, length us, event | category | flops | bytes accessed | tf_op | source)
XLA Modules:
  0.0 123.8 jit_solution(11042238857782505655)
XLA Ops:
  0.0 121.9 %shard_map.64 = f32[4,64,512]{2,1,0:T(8,128)} custom-call(bf16[256,1024]{1,0:T(8,128)(2,1)} %chol_hbm.1, bf16[256,1024]{1,0:T(8,128)(2,1)} %bitcast.5, f32[8,128]{1,0:T(8,128)} %bitcast.6, bf16[8192,512]{1,0:T(8,128)(2,1)} %trade_hbm.1, bf16[64,8192]{1,0:T(8,128)(2,1)} %bitcast.4, s32[1,512]{1,0:T(1,128)} %bitcast.7), custom_call_target="tpu_custom_call" | custom-call | tf_op jit(solution)/shard_map/pallas_call | solution.py:568
  121.9 1.9 %copy.8 = f32[4,64,512]{2,1,0:T(8,128)} copy(f32[4,64,512]{2,1,0:T(8,128)} %shard_map.64) | data formatting | bytes 1048576
